TPU v7x, 32 devices: a whole 2x2x4 slice. The times are simulated.
32 devices in a mesh: segment: 2 (over core), expert: 8 (over z, y), dp: 2 (over x).
Axes of the slice: x: 2, y: 2, z: 4, core: 2. Of those that a mesh axis runs over, the one named last changes fastest.
Arguments:
- moe_input: bfloat16 [2, 1024, 2688], P('segment', 'expert', 'dp'), may hold values from -64 to 64
- norm_gain: float32 [2688], replicated, may hold values from 0.1 to 1.9
- routes: int32 [2, 1024, 6], P('segment', 'expert'), may hold values from 0 to 15, all different within a row; in each aligned block of 128 rows (0 to 127, 128 to 255, ..., all dimensions but the last counted through in order) at most 54 rows name the same one
- route_scores: float32 [2, 1024, 6], P('segment', 'expert'), may hold values from -8 to 8
- w_up: bfloat16 [16, 2688, 1856], P('expert', None, 'dp'), may hold values from -0.125 to 0.125
- w_down: bfloat16 [16, 1856, 2688], P('expert', None, 'dp'), may hold values from -0.125 to 0.125
- queries: bfloat16 [2, 1024, 2048], P('segment', 'expert', 'dp'), may hold values from -100 to 100
- keys: bfloat16 [2, 1024, 256], P('segment', 'expert'), may hold values from -6 to 6
- values: bfloat16 [2, 1024, 256], P('segment', 'expert'), may hold values from -6 to 6
- out_grad: bfloat16 [2, 1024, 2688], P('segment', 'expert'), may hold values from -6 to 6
- w_query: bfloat16 [2688, 2048], P(None, 'dp'), may hold values from -0.125 to 0.125
- w_key: bfloat16 [2688, 256], replicated, may hold values from -0.125 to 0.125
- w_value: bfloat16 [2688, 256], replicated, may hold values from -0.125 to 0.125
- w_out: bfloat16 [2048, 2688], P('dp'), may hold values from -0.125 to 0.125
Outputs:
- moe_next: bfloat16 [2, 1024, 2688], P('segment', 'expert', 'dp')
- grad_prev: bfloat16 [2, 1024, 2688], P('segment', 'expert', 'dp')
Inputs may be any that keep to these rules, and one draw needn't show every extreme that they name: `routes`: each row names 6 different experts. Among the 128 rows of one sequence no expert is named more than 54 times, a bound that some block reaches; every expert is named by some row.
All inputs are finite; a program needn't handle non-finite values.
Results may differ from a plain program's by a relative error of at most 0.028.
Values may be sent and summed in bfloat16 or wider, within the bound.
No kernel may reach another device: no remote copies, remote signals or barrier semaphores. Data moves between devices by JAX's collectives and lax.ppermute only.
A program may use at most 128 MiB of HBM per device.

v0:
```python
import jax
import jax.numpy as jnp
from jax import lax
from jax.sharding import PartitionSpec as P

D = 2688
HEADS = 16
KV_HEADS = 2
HEAD_DIM = 128
TOPK = 6
NORM_EPSILON = 1e-05


def partner(block, axis, distance):
    count = lax.axis_size(axis)
    route = []
    for low in range(count):
        high = low | 1 << distance
        if high != low and high < count:
            route += [(low, high), (high, low)]
    return lax.ppermute(block, axis, route)


def attention_grad(queries, keys, values, out_grad, w_query, w_key, w_value, w_out, block_index):
    token_count = queries.shape[0]
    query_width = queries.shape[1]
    heads_here = query_width // HEAD_DIM
    group_size = HEADS // KV_HEADS
    score_scale = HEAD_DIM ** (-0.5)
    head_group = block_index * heads_here // group_size
    kv_start = head_group * HEAD_DIM
    key_head = lax.dynamic_slice_in_dim(keys, kv_start, HEAD_DIM, 1)
    value_head = lax.dynamic_slice_in_dim(values, kv_start, HEAD_DIM, 1)
    key_weight = lax.dynamic_slice_in_dim(w_key, kv_start, HEAD_DIM, 1)
    value_weight = lax.dynamic_slice_in_dim(w_value, kv_start, HEAD_DIM, 1)
    d_attn = jnp.einsum("td,qd->tq", out_grad, w_out, preferred_element_type=jnp.float32).astype(
        jnp.bfloat16
    )
    grad_heads = d_attn.reshape(token_count, heads_here, HEAD_DIM)
    query_heads = queries.reshape(token_count, heads_here, HEAD_DIM)
    scores = (
        jnp.einsum("ihd,jd->hij", query_heads, key_head, preferred_element_type=jnp.float32)
        * score_scale
    )
    positions = jnp.arange(token_count, dtype=jnp.int32)
    causal = positions[None, :] <= positions[:, None]
    scores = jnp.where(causal[None], scores, -jnp.inf)
    peak = jnp.max(scores, axis=2, keepdims=True)
    raised = jnp.exp(scores - peak)
    attn_weights = raised / jnp.sum(raised, axis=2, keepdims=True)
    d_weights = jnp.einsum(
        "ihd,jd->hij", grad_heads, value_head, preferred_element_type=jnp.float32
    )
    row_delta = jnp.sum(attn_weights * d_weights, axis=2, keepdims=True)
    d_scores = (attn_weights * (d_weights - row_delta)).astype(jnp.bfloat16)
    d_query = (
        jnp.einsum("hij,jd->ihd", d_scores, key_head, preferred_element_type=jnp.float32)
        * score_scale
    )
    d_query = d_query.astype(jnp.bfloat16).reshape(token_count, query_width)
    d_key = (
        jnp.einsum("hij,ihd->jd", d_scores, query_heads, preferred_element_type=jnp.float32)
        * score_scale
    ).astype(jnp.bfloat16)
    d_value = jnp.einsum(
        "hij,ihd->jd",
        attn_weights.astype(jnp.bfloat16),
        grad_heads,
        preferred_element_type=jnp.float32,
    ).astype(jnp.bfloat16)
    grad_term = jnp.einsum("tq,dq->td", d_query, w_query, preferred_element_type=jnp.float32)
    grad_term = grad_term + jnp.einsum(
        "tk,dk->td", d_key, key_weight, preferred_element_type=jnp.float32
    )
    grad_term = grad_term + jnp.einsum(
        "tk,dk->td", d_value, value_weight, preferred_element_type=jnp.float32
    )
    return grad_term


def block_product(block_rows, w_up, first_feature):
    width = block_rows.shape[3]
    weight_rows = lax.dynamic_slice_in_dim(w_up, first_feature, width, 1)
    product = jnp.einsum(
        "sjcw,jwh->sjch", block_rows, weight_rows, preferred_element_type=jnp.float32
    )
    return lax.optimization_barrier(product.astype(jnp.bfloat16)).astype(jnp.float32)


def on_device(
    moe_input,
    norm_gain,
    routes,
    route_scores,
    w_up,
    w_down,
    queries,
    keys,
    values,
    out_grad,
    w_query,
    w_key,
    w_value,
    w_out,
):
    columns = lax.axis_size("expert")
    token_count = moe_input.shape[1]
    feature_share = moe_input.shape[2]
    local_experts = w_up.shape[0]
    hidden_share = w_up.shape[2]
    expert_count = local_experts * columns
    capacity = (9 * token_count * TOPK + 8 * expert_count - 1) // (8 * expert_count)
    slot_count = expert_count * capacity
    feature_index = lax.axis_index("dp")
    token_rows = moe_input[0]
    chosen_experts = routes[0]
    logits = route_scores[0]
    flat_choices = chosen_experts.reshape(-1)
    expert_hits = (
        flat_choices[:, None] == jnp.arange(expert_count, dtype=jnp.int32)[None, :]
    ).astype(jnp.int32)
    earlier = jnp.cumsum(expert_hits, axis=0) - expert_hits
    places = jnp.sum(earlier * expert_hits, axis=1).reshape(token_count, TOPK)
    targets = chosen_experts * capacity + places
    slot_ids = jnp.arange(slot_count, dtype=jnp.int32)
    signal = jax.nn.sigmoid(logits)
    gate_values = (
        (signal / jnp.sum(signal, axis=1, keepdims=True)).astype(jnp.bfloat16).astype(jnp.float32)
    )
    spread_sum = jnp.zeros((token_count, slot_count), jnp.float32)
    mixing_sum = jnp.zeros((token_count, slot_count), jnp.float32)
    for choice_index in range(TOPK):
        hit = slot_ids[None, :] == targets[:, choice_index : choice_index + 1]
        spread_sum = spread_sum + hit.astype(jnp.float32)
        mixing_sum = mixing_sum + jnp.where(
            hit, gate_values[:, choice_index : choice_index + 1], 0.0
        )
    spread = spread_sum.astype(jnp.bfloat16)
    mixing = mixing_sum.astype(jnp.bfloat16)
    outgoing = jnp.einsum(
        "ts,tw->sw", spread, token_rows, preferred_element_type=jnp.float32
    ).astype(jnp.bfloat16)
    outgoing = outgoing.reshape(columns, local_experts, capacity, feature_share)
    arrived = lax.all_to_all(outgoing, "expert", split_axis=0, concat_axis=0, tiled=True)
    arrived_wide = arrived.astype(jnp.float32)
    start_up = jnp.zeros((columns, local_experts, capacity, hidden_share), jnp.float32)
    squares = lax.psum(jnp.sum(jnp.square(arrived_wide), axis=3), "dp")
    gain_part = lax.dynamic_slice_in_dim(norm_gain, feature_index * feature_share, feature_share, 0)
    scaled = (arrived_wide * gain_part).astype(jnp.bfloat16)
    running = start_up
    piece = lax.all_gather(scaled, "dp", axis=3, tiled=True)
    start = jnp.int32(0)
    for block_number in range(piece.shape[3] // feature_share):
        first = block_number * feature_share
        running = running + block_product(
            piece[:, :, :, first : first + feature_share], w_up, start + first
        )
    inverse = 1.0 / jnp.sqrt(squares / D + NORM_EPSILON)
    projected = running * inverse[..., None]
    hidden = jnp.square(jnp.maximum(projected, 0.0)).astype(jnp.bfloat16)
    grad_term = attention_grad(
        queries[0], keys[0], values[0], out_grad[0], w_query, w_key, w_value, w_out, feature_index
    )
    grad_here = lax.psum_scatter(
        grad_term.astype(jnp.bfloat16), "dp", scatter_dimension=1, tiled=True
    )
    expert_out = jnp.einsum(
        "sjch,jhd->sjcd",
        lax.all_gather(hidden, "dp", axis=3, tiled=True),
        w_down,
        preferred_element_type=jnp.float32,
    )
    expert_rows = expert_out.astype(jnp.bfloat16)
    returned = lax.all_to_all(expert_rows, "expert", split_axis=0, concat_axis=0, tiled=True)
    moe_out = jnp.dot(
        mixing, returned.reshape(slot_count, feature_share), preferred_element_type=jnp.float32
    ).astype(jnp.bfloat16)
    moe_next, grad_prev = partner((moe_out, grad_here), "segment", 0)
    return (moe_next[None], grad_prev[None])


def solution(mesh):
    return jax.shard_map(
        on_device,
        mesh=mesh,
        in_specs=(
            P("segment", "expert", "dp"),
            P(),
            P("segment", "expert", None),
            P("segment", "expert", None),
            P("expert", None, "dp"),
            P("expert", None, "dp"),
            P("segment", "expert", "dp"),
            P("segment", "expert", None),
            P("segment", "expert", None),
            P("segment", "expert", None),
            P(None, "dp"),
            P(),
            P(),
            P("dp", None),
        ),
        out_specs=(P("segment", "expert", "dp"), P("segment", "expert", "dp")),
        check_vma=False,
    )
```

profile of v0, /device:TPU:0, one launch (start us, length us, event | category | flops | bytes accessed | tf_op | source)
XLA Modules:
  0.0 497.4 jit_solution(2547123518346177844)
XLA Ops:
  11.5 3.5 convolution_convert_fusion
  15.0 21.9 %reshape.76 = bf16[8,2,54,1344]{2,1,0,3:T(2,128)(2,1)} reshape(bf16[864,1344]{0,1:T(8,128)(2,1)} %convolution_convert_fusion) | data formatting | bytes 4644864 | tf_op jit(solution)/shard_map/reshape | solution.py:143
  36.8 15.1 %copy.87 = bf16[8,2,54,1344]{3,1,2,0:T(2,128)(2,1)} copy(bf16[8,2,54,1344]{2,1,0,3:T(2,128)(2,1)} %reshape.76) | data formatting | bytes 4644864 | tf_op jit(solution)/shard_map/reshape | solution.py:143
  52.0 7.4 %all-to-all-start = ((bf16[8,2,54,1344]{3,1,2,0:T(2,128)(2,1)}), bf16[8,2,54,1344]{3,1,2,0:T(2,128)(2,1)}, u32[]{:S(2)}, u32[]{:S(2)}) async-start(bf16[8,2,54,1344]{3,1,2,0:T(2,128)(2,1)} %copy.87), calls=%async_computation | async-start | bytes 4866048 | tf_op jit(solution)/shard_map/all_to_all | solution.py:144
  59.5 55.4 %all-to-all-done = bf16[8,2,54,1344]{3,1,2,0:T(2,128)(2,1)} async-done(((bf16[8,2,54,1344]{3,1,2,0:T(2,128)(2,1)}), bf16[8,2,54,1344]{3,1,2,0:T(2,128)(2,1)}, u32[]{:S(2)}, u32[]{:S(2)}) %all-to-all-start) | async-done | bytes 2322464 | tf_op jit(solution)/shard_map/all_to_all | solution.py:144
  114.9 3.9 fusion.13
  118.8 8.9 %copy.89 = bf16[8,2,54,1344]{2,0,1,3:T(8,128)(2,1)} copy(bf16[8,2,54,1344]{3,0,2,1:T(8,128)(2,1)} %get-tuple-element.11) | data formatting | bytes 4644864 | tf_op jit(solution)/shard_map/convert_element_type | solution.py:149
  127.9 5.0 psum.7
  132.9 129.3 %all-gather.3.cloned.1.call-done = bf16[8,2,54,2688]{2,0,1,3:T(8,128)(2,1)} async-done(((bf16[8,2,54,1344]{2,0,1,3:T(8,128)(2,1)}), bf16[8,2,54,2688]{2,0,1,3:T(8,128)(2,1)}) %all-gather.3.cloned.1.call-update) | async-done | bytes 4644880 | tf_op jit(solution)/shard_map/all_gather | solution.py:151
  262.2 5.5 %fusion.112 = (bf16[8,2,54,1344]{2,0,1,3:T(8,128)(2,1)S(1)}, bf16[8,2,54,1344]{2,0,1,3:T(8,128)(2,1)S(1)}) fusion(bf16[8,2,54,2688]{2,0,1,3:T(8,128)(2,1)} %all-gather.3.cloned.1.call-done), kind=kLoop, calls=%fused_computation.132 | loop fusion | bytes 9289728 | tf_op jit(solution)/shard_map/slice | solution.py:156
  267.7 11.1 %convert_bitcast_fusion.1 = bf16[8,2,54,928]{3,2,0,1:T(8,128)(2,1)} fusion(bf16[2,2688,928]{1,2,0:T(8,128)(2,1)} %param.18, bf16[8,2,54,1344]{2,0,1,3:T(8,128)(2,1)S(1)} %get-tuple-element.8), kind=kOutput, calls=%fused_computation.25 | convolution fusion | flops 2156018688 | bytes 9152512 | tf_op jit(solution)/shard_map/sjcw,jwh->sjch/dot_general | solution.py:84
  278.9 10.0 %convert_bitcast_fusion = bf16[8,2,54,928]{3,2,0,1:T(8,128)(2,1)S(1)} fusion(bf16[2,2688,928]{1,2,0:T(8,128)(2,1)} %param.18, bf16[8,2,54,1344]{2,0,1,3:T(8,128)(2,1)S(1)} %get-tuple-element.9), kind=kOutput, calls=%fused_computation.24 | convolution fusion | flops 2156018688 | bytes 9152512 | tf_op jit(solution)/shard_map/sjcw,jwh->sjch/dot_general | solution.py:84
  289.7 4.9 copy.94
  294.7 95.3 %all-gather.5.cloned.1.call-done = bf16[8,2,54,1856]{2,0,1,3:T(8,128)(2,1)} async-done(((bf16[8,2,54,928]{2,0,1,3:T(8,128)(2,1)}), bf16[8,2,54,1856]{2,0,1,3:T(8,128)(2,1)}) %all-gather.5.cloned.1.call-update) | async-done | bytes 3207184 | tf_op jit(solution)/shard_map/all_gather | solution.py:169
  389.9 20.2 %fusion.20 = bf16[8,2,54,1344]{3,2,0,1:T(8,128)(2,1)} fusion(bf16[2,1856,1344]{1,2,0:T(8,128)(2,1)} %param.19, bf16[8,2,54,1856]{2,0,1,3:T(8,128)(2,1)} %all-gather.5.cloned.1.call-done), kind=kOutput, calls=%fused_computation.22 | convolution fusion | flops 4311595008 | bytes 15507456 | tf_op jit(solution)/shard_map/sjch,jhd->sjcd/dot_general | solution.py:167
  410.1 5.7 %copy.96 = bf16[8,2,54,1344]{3,1,2,0:T(2,128)(2,1)} copy(bf16[8,2,54,1344]{3,2,0,1:T(8,128)(2,1)} %fusion.20) | data formatting | bytes 4644864 | tf_op jit(solution)/shard_map/convert_element_type | solution.py:173
  415.8 5.6 %all-to-all-start.1 = ((bf16[8,2,54,1344]{3,1,2,0:T(2,128)(2,1)}), bf16[8,2,54,1344]{3,1,2,0:T(2,128)(2,1)}, u32[]{:S(2)}, u32[]{:S(2)}) async-start(bf16[8,2,54,1344]{3,1,2,0:T(2,128)(2,1)} %copy.96), calls=%async_computation.1 | async-start | bytes 4866048 | tf_op jit(solution)/shard_map/all_to_all | solution.py:174
  422.2 4.4 fusion.38
  429.6 4.6 convolution_add_fusion
  436.9 16.7 %reduce-scatter.2.cloned.1.call-done = bf16[128,1344]{0,1:T(8,128)(2,1)} async-done(((bf16[128,2688]{0,1:T(8,128)(2,1)}), bf16[128,1344]{0,1:T(8,128)(2,1)}) %reduce-scatter.2.cloned.1.call-update) | async-done | bytes 344080 | tf_op jit(solution)/shard_map/reduce_scatter | solution.py:164
  453.5 23.2 %all-to-all-done.1 = bf16[8,2,54,1344]{3,1,2,0:T(2,128)(2,1)} async-done(((bf16[8,2,54,1344]{3,1,2,0:T(2,128)(2,1)}), bf16[8,2,54,1344]{3,1,2,0:T(2,128)(2,1)}, u32[]{:S(2)}, u32[]{:S(2)}) %all-to-all-start.1) | async-done | bytes 2322464 | tf_op jit(solution)/shard_map/all_to_all | solution.py:174
  476.8 3.5 copy.97
  480.3 4.4 reshape.65
  484.7 3.0 convolution_convert_fusion.1
  (71 shorter events, 14.7 us)
Async XLA Ops:
  7.2 420.8 %copy-start = (bf16[2688,256]{1,0:T(8,128)(2,1)S(1)}, bf16[2688,256]{1,0:T(8,128)(2,1)}, u32[]{:S(2)}) copy-start(bf16[2688,256]{1,0:T(8,128)(2,1)} %param.25) | copy-start | bytes 4128772
  10.9 0.5 copy-start.7
  10.9 0.5 copy-start.9
  10.9 0.5 copy-start.11
  11.0 0.6 copy-start.13
  51.9 7.5 %copy-start.5 = (f32[2688]{0:T(1024)S(1)}, f32[2688]{0:T(1024)}, u32[]{:S(2)}) copy-start(f32[2688]{0:T(1024)} %param.15) | copy-start | bytes 32260
  52.0 63.0 %all-to-all-start = ((bf16[8,2,54,1344]{3,1,2,0:T(2,128)(2,1)}), bf16[8,2,54,1344]{3,1,2,0:T(2,128)(2,1)}, u32[]{:S(2)}, u32[]{:S(2)}) async-start(bf16[8,2,54,1344]{3,1,2,0:T(2,128)(2,1)} %copy.87), calls=%async_computation | async-start | bytes 4866048 | tf_op jit(solution)/shard_map/all_to_all | solution.py:144
  59.4 202.8 %all-gather.3.cloned.1.call-start = ((), (), s32[]{:S(2)}) async-start(), calls=%async_computation.3 | async-start | bytes 16515072 | tf_op jit(solution)/shard_map/all_gather | solution.py:151
  127.8 262.2 %all-gather.5.cloned.1.call-start = ((), (), s32[]{:S(2)}) async-start(), calls=%async_computation.4 | async-start | bytes 11403264 | tf_op jit(solution)/shard_map/all_gather | solution.py:169
  278.9 10.1 %copy-start.1 = (bf16[8,2,54,928]{3,2,0,1:T(8,128)(2,1)S(1)}, bf16[8,2,54,928]{3,2,0,1:T(8,128)(2,1)}, u32[]{:S(2)}) copy-start(bf16[8,2,54,928]{3,2,0,1:T(8,128)(2,1)} %convert_bitcast_fusion.1) | copy-start | bytes 4810756
  415.8 6.0 %copy-start.3 = (bf16[1,128,1024]{2,1,0:T(8,128)(2,1)S(1)}, bf16[1,128,1024]{2,1,0:T(8,128)(2,1)}, u32[]{:S(2)}) copy-start(bf16[1,128,1024]{2,1,0:T(8,128)(2,1)} %param.20) | copy-start | bytes 786436
  415.8 6.1 %copy-start.4 = (bf16[1,128,256]{2,1,0:T(8,128)(2,1)S(1)}, bf16[1,128,256]{2,1,0:T(8,128)(2,1)}, u32[]{:S(2)}) copy-start(bf16[1,128,256]{2,1,0:T(8,128)(2,1)} %param.21) | copy-start | bytes 196612
  415.8 6.4 %copy-start.2 = (bf16[1,128,2688]{2,1,0:T(8,128)(2,1)S(1)}, bf16[1,128,2688]{2,1,0:T(8,128)(2,1)}, u32[]{:S(2)}) copy-start(bf16[1,128,2688]{2,1,0:T(8,128)(2,1)} %param.23) | copy-start | bytes 2064388
  415.8 61.0 %all-to-all-start.1 = ((bf16[8,2,54,1344]{3,1,2,0:T(2,128)(2,1)}), bf16[8,2,54,1344]{3,1,2,0:T(2,128)(2,1)}, u32[]{:S(2)}, u32[]{:S(2)}) async-start(bf16[8,2,54,1344]{3,1,2,0:T(2,128)(2,1)} %copy.96), calls=%async_computation.1 | async-start | bytes 4866048 | tf_op jit(solution)/shard_map/all_to_all | solution.py:174
  421.4 32.1 %reduce-scatter.2.cloned.1.call-start = ((), (), s32[]{:S(2)}) async-start(), calls=%async_computation.5 | async-start | bytes 1032192 | tf_op jit(solution)/shard_map/reduce_scatter | solution.py:164
  421.8 4.8 copy-start.15
  434.2 2.6 copy-start.6
  453.5 34.3 %collective-permute-start.1 = (bf16[128,1344]{0,1:T(8,128)(2,1)}, bf16[128,1344]{0,1:T(8,128)(2,1)S(1)}, u32[]{:S(2)}, u32[]{:S(2)}) collective-permute-start(bf16[128,1344]{0,1:T(8,128)(2,1)} %reduce-scatter.2.cloned.1.call-done), channel_id=1, source_target_pairs={{0,16},{16,0},{1,17},{17,1},{2,18},{18,2},{3,19},{19,3},{4,20},{20... | collective-permute-start | bytes 1032200 | tf_op jit(solution)/shard_map/ppermute | solution.py:21
  480.3 4.4 copy-start.8
  480.3 4.4 copy-start.10
  480.3 4.4 copy-start.12
  480.3 4.4 copy-start.14
  487.7 1.7 collective-permute-start
Sparse Core Ops, SparseCore 0:
  127.9 134.2 all-gather.2
  294.8 95.1 all-gather.4
  436.9 16.5 reduce-scatter.1
where the time goes:
time: 499 us; the launch traced here: 497 us
  waiting for transfers between devices  322 us (65%)
  local copies, waits for them, and re-layouts  74 us (15%)
  matrix products  62.6 us (13%)
  between operations  14.1 us (3%)
  starting transfers between devices  13.5 us (3%)
  other arithmetic  6.66 us (1%)
    all_gather x1, waiting for transfers between devices, on_device(): piece = lax.all_gather(scaled, 'dp', axis=3, tiled=True)  129 us
    all_gather x1, waiting for transfers between devices, on_device(): lax.all_gather(hidden, 'dp', axis=3, tiled=True)  95.3 us
    all_to_all x1, waiting for transfers between devices, on_device(): lax.all_to_all(outgoing, 'expert', split_axis=0, concat_axis=0, tiled=True)  55.4 us
    reshape x2, local copies, waits for them, and re-layouts, on_device(): outgoing = outgoing.reshape(columns, local_experts, capacity, feature_share)  37 us
    all_to_all x1, waiting for transfers between devices, on_device(): lax.all_to_all(expert_rows, 'expert', split_axis=0, concat_axis=0, tiled=...  23.2 us
    dot_general x2, matrix products, block_product(): jnp.einsum('sjcw,jwh->sjch', block_rows, weight_rows, preferred_element_t...  21.2 us
    dot_general x1, matrix products, on_device(): jnp.einsum('sjch,jhd->sjcd', lax.all_gather(hidden, 'dp', axis=3, tiled=T...  20.2 us
    reduce_scatter x1, waiting for transfers between devices, on_device(): lax.psum_scatter(grad_term.astype(jnp.bfloat16), 'dp', scatter_dimension=...  16.7 us
  transfers between devices with their start and end apart: 7, of which 6 were waited for; matrix products, arithmetic and copies ran while one was open for 5% of the time, Pallas kernels for 0%

commit v1 on v0

--- a/solution.py
+++ b/solution.py
@@ -9,6 +9,18 @@
 HEAD_DIM = 128
 TOPK = 6
 NORM_EPSILON = 1e-05
+
+
+def gather_by_bits(value, axis, dim):
+    ways, here = (lax.axis_size(axis), lax.axis_index(axis))
+    grown, reach = (value, 1)
+    while reach < ways:
+        theirs = lax.ppermute(grown, axis, [(d, d ^ reach) for d in range(ways)])
+        mine_first = jnp.concatenate([grown, theirs], axis=dim)
+        theirs_first = jnp.concatenate([theirs, grown], axis=dim)
+        grown = jnp.where(here & reach == 0, mine_first, theirs_first)
+        reach = 2 * reach
+    return grown
 
 
 def partner(block, axis, distance):
@@ -148,7 +160,7 @@
     gain_part = lax.dynamic_slice_in_dim(norm_gain, feature_index * feature_share, feature_share, 0)
     scaled = (arrived_wide * gain_part).astype(jnp.bfloat16)
     running = start_up
-    piece = lax.all_gather(scaled, "dp", axis=3, tiled=True)
+    piece = gather_by_bits(scaled, "dp", 3)
     start = jnp.int32(0)
     for block_number in range(piece.shape[3] // feature_share):
         first = block_number * feature_share

time: 499 us -> 401 us (0.80)
  waiting for transfers between devices: 322 us -> 193 us
  blocking collectives: 4.96 us -> 52.4 us
  matrix products: 62.6 us -> 50.9 us
  local copies, waits for them, and re-layouts: 74 us -> 65.1 us
    all_gather x1 -> x0, waiting for transfers between devices: 129 us -> none  [on_device(): piece = lax.all_gather(scaled, 'dp', axis=3, tiled=True)]
    psum x1, blocking collectives: 4.96 us -> 52.4 us  [on_device(): squares = lax.psum(jnp.sum(jnp.square(arrived_wide), axis=3), 'dp')]
    dot_general x2, matrix products: 21.2 us -> 9.48 us  [block_product(): jnp.einsum('sjcw,jwh->sjch', block_rows, weight_rows, preferred_element_t...]
    convert_element_type x1, local copies, waits for them, and re-layouts: 8.93 us -> 1.72 us  [on_device(): scaled = (arrived_wide * gain_part).astype(jnp.bfloat16)]
    slice x2 -> x1, local copies, waits for them, and re-layouts: 5.75 us -> 0.25 us  [the longest x1 5.5 us: on_device(): piece[:, :, :, first:first + feature_share]]
  transfers between devices with their start and end apart: 7 -> 7, of which waited for: 6 -> 5; matrix products, arithmetic and copies ran while one was open for 5% -> 6% of each run, Pallas kernels for 0% -> 0%
where the time goes in v1:
time: 401 us; the launch traced here: 400 us
  waiting for transfers between devices  193 us (48%)
  local copies, waits for them, and re-layouts  65.1 us (16%)
  blocking collectives  52.4 us (13%)
  matrix products  50.9 us (13%)
  starting transfers between devices  15 us (4%)
  between operations  14.4 us (4%)
  other arithmetic  10 us (2%)
    all_gather x1, waiting for transfers between devices, on_device(): lax.all_gather(hidden, 'dp', axis=3, tiled=True)  95.6 us
    all_to_all x1, waiting for transfers between devices, on_device(): lax.all_to_all(outgoing, 'expert', split_axis=0, concat_axis=0, tiled=True)  55.4 us
    psum x1, blocking collectives, on_device(): squares = lax.psum(jnp.sum(jnp.square(arrived_wide), axis=3), 'dp')  52.4 us
    reshape x2, local copies, waits for them, and re-layouts, on_device(): outgoing = outgoing.reshape(columns, local_experts, capacity, feature_share)  37 us
    all_to_all x1, waiting for transfers between devices, on_device(): lax.all_to_all(expert_rows, 'expert', split_axis=0, concat_axis=0, tiled=...  23.2 us
    dot_general x1, matrix products, on_device(): jnp.einsum('sjch,jhd->sjcd', lax.all_gather(hidden, 'dp', axis=3, tiled=T...  20.2 us
    reduce_scatter x1, waiting for transfers between devices, on_device(): lax.psum_scatter(grad_term.astype(jnp.bfloat16), 'dp', scatter_dimension=...  16.7 us
    dot_general x2, matrix products, block_product(): jnp.einsum('sjcw,jwh->sjch', block_rows, weight_rows, preferred_element_t...  9.48 us
  transfers between devices with their start and end apart: 7, of which 5 were waited for; matrix products, arithmetic and copies ran while one was open for 6% of the time, Pallas kernels for 0%

profile of v1, /device:TPU:0, one launch (start us, length us, event | category | flops | bytes accessed | tf_op | source)
XLA Modules:
  0.0 400.4 jit_solution(7664096428616999825)
XLA Ops:
  11.5 3.5 convolution_convert_fusion
  15.0 21.9 %reshape.76 = bf16[8,2,54,1344]{2,1,0,3:T(2,128)(2,1)} reshape(bf16[864,1344]{0,1:T(8,128)(2,1)} %convolution_convert_fusion) | data formatting | bytes 4644864 | tf_op jit(solution)/shard_map/reshape | solution.py:155
  36.9 15.1 %copy.48 = bf16[8,2,54,1344]{3,1,2,0:T(2,128)(2,1)} copy(bf16[8,2,54,1344]{2,1,0,3:T(2,128)(2,1)} %reshape.76) | data formatting | bytes 4644864 | tf_op jit(solution)/shard_map/reshape | solution.py:155
  52.0 7.4 %all-to-all-start = ((bf16[8,2,54,1344]{3,1,2,0:T(2,128)(2,1)}), bf16[8,2,54,1344]{3,1,2,0:T(2,128)(2,1)}, u32[]{:S(2)}, u32[]{:S(2)}) async-start(bf16[8,2,54,1344]{3,1,2,0:T(2,128)(2,1)} %copy.48), calls=%async_computation | async-start | bytes 4866048 | tf_op jit(solution)/shard_map/all_to_all | solution.py:156
  59.5 55.4 %all-to-all-done = bf16[8,2,54,1344]{3,1,2,0:T(2,128)(2,1)} async-done(((bf16[8,2,54,1344]{3,1,2,0:T(2,128)(2,1)}), bf16[8,2,54,1344]{3,1,2,0:T(2,128)(2,1)}, u32[]{:S(2)}, u32[]{:S(2)}) %all-to-all-start) | async-done | bytes 2322464 | tf_op jit(solution)/shard_map/all_to_all | solution.py:156
  115.0 2.6 fusion.11
  122.2 52.4 %psum.7 = f32[8,2,54]{2,0,1:T(8,128)S(1)} all-reduce(f32[8,2,54]{2,0,1:T(8,128)S(1)} %get-tuple-element.8), channel_id=1, replica_groups=mesh['segment'=2,'expert'=8,'dp'=2] {'dp'}, use_global_device_ids=true, to_apply=%region_5.6 | all-reduce | flops 864 | bytes 6912 | tf_op jit(solution)/shard_map/psum | solution.py:159
  174.6 2.1 copy.51
  177.0 4.7 %maximum_select_fusion = bf16[8,2,54,2688]{3,2,0,1:T(8,128)(2,1)S(1)} fusion(bf16[8,2,54,1344]{3,2,0,1:T(8,128)(2,1)S(1)} %copy.51, bf16[8,2,54,1344]{3,2,0,1:T(8,128)(2,1)S(1)} %copy-done.2, pred[]{:T(512)S(6)} %eq.150), kind=kLoop, calls=%fused_computation.14 | loop fusion | flops 20901888 | bytes 9289729 | tf_op jit(solution)/shard_map/jit(_where)/select_n | solution.py:21
  181.8 5.6 %convert_bitcast_fusion.1 = bf16[8,2,54,928]{3,2,0,1:T(8,128)(2,1)S(1)} fusion(bf16[2,2688,928]{1,2,0:T(8,128)(2,1)} %param.18, bf16[8,2,54,2688]{3,2,0,1:T(8,128)(2,1)S(1)} %maximum_select_fusion), kind=kOutput, calls=%fused_computation.26 | convolution fusion | flops 2156018688 | bytes 9353216 | tf_op jit(solution)/shard_map/sjcw,jwh->sjch/dot_general | solution.py:96
  187.4 3.8 convert_bitcast_fusion
  192.1 4.9 %copy.53 = bf16[8,2,54,928]{2,0,1,3:T(8,128)(2,1)} copy(bf16[8,2,54,928]{3,2,0,1:T(8,128)(2,1)S(1)} %multiply_convert_fusion) | data formatting | bytes 3207168 | tf_op jit(solution)/shard_map/convert_element_type | solution.py:172
  197.0 95.6 %all-gather.2.cloned.1.call-done = bf16[8,2,54,1856]{2,0,1,3:T(8,128)(2,1)} async-done(((bf16[8,2,54,928]{2,0,1,3:T(8,128)(2,1)}), bf16[8,2,54,1856]{2,0,1,3:T(8,128)(2,1)}) %all-gather.2.cloned.1.call-update) | async-done | bytes 3207184 | tf_op jit(solution)/shard_map/all_gather | solution.py:181
  292.6 20.2 %fusion.18 = bf16[8,2,54,1344]{3,2,0,1:T(8,128)(2,1)} fusion(bf16[2,1856,1344]{1,2,0:T(8,128)(2,1)} %param.19, bf16[8,2,54,1856]{2,0,1,3:T(8,128)(2,1)} %all-gather.2.cloned.1.call-done), kind=kOutput, calls=%fused_computation.21 | convolution fusion | flops 4311595008 | bytes 15507456 | tf_op jit(solution)/shard_map/sjch,jhd->sjcd/dot_general | solution.py:179
  312.8 5.7 %copy.55 = bf16[8,2,54,1344]{3,1,2,0:T(2,128)(2,1)} copy(bf16[8,2,54,1344]{3,2,0,1:T(8,128)(2,1)} %fusion.18) | data formatting | bytes 4644864 | tf_op jit(solution)/shard_map/convert_element_type | solution.py:185
  318.4 5.6 %all-to-all-start.1 = ((bf16[8,2,54,1344]{3,1,2,0:T(2,128)(2,1)}), bf16[8,2,54,1344]{3,1,2,0:T(2,128)(2,1)}, u32[]{:S(2)}, u32[]{:S(2)}) async-start(bf16[8,2,54,1344]{3,1,2,0:T(2,128)(2,1)} %copy.55), calls=%async_computation.1 | async-start | bytes 4866048 | tf_op jit(solution)/shard_map/all_to_all | solution.py:186
  324.9 4.4 %fusion.38 = bf16[16,8,8,128]{3,2,1,0:T(8,128)(2,1)S(1)} fusion(bf16[1024,2688]{1,0:T(8,128)(2,1)} %param.27, bf16[1,128,2688]{2,1,0:T(8,128)(2,1)S(1)} %copy-done.3), kind=kOutput, calls=%fused_computation.36 | convolution fusion | flops 704774144 | bytes 6455296 | tf_op jit(solution)/shard_map/td,qd->tq/dot_general | solution.py:48
  332.3 4.6 %convolution_add_fusion = f32[128,2688]{0,1:T(8,128)S(1)} fusion(f32[128,2688]{0,1:T(8,128)} %fusion.42, bf16[2688,1024]{1,0:T(8,128)(2,1)} %param.24, bf16[128,1024]{0,1:T(8,128)(2,1)} %bitcast.152), kind=kOutput, calls=%fused_computation.15 | convolution fusion | flops 704987136 | bytes 8519680 | tf_op jit(solution)/shard_map/tq,dq->td/dot_general | solution.py:83
  336.9 2.5 fusion.12
  339.6 16.7 %reduce-scatter.2.cloned.1.call-done = bf16[128,1344]{0,1:T(8,128)(2,1)} async-done(((bf16[128,2688]{0,1:T(8,128)(2,1)}), bf16[128,1344]{0,1:T(8,128)(2,1)}) %reduce-scatter.2.cloned.1.call-update) | async-done | bytes 344080 | tf_op jit(solution)/shard_map/reduce_scatter | solution.py:176
  356.2 23.2 %all-to-all-done.1 = bf16[8,2,54,1344]{3,1,2,0:T(2,128)(2,1)} async-done(((bf16[8,2,54,1344]{3,1,2,0:T(2,128)(2,1)}), bf16[8,2,54,1344]{3,1,2,0:T(2,128)(2,1)}, u32[]{:S(2)}, u32[]{:S(2)}) %all-to-all-start.1) | async-done | bytes 2322464 | tf_op jit(solution)/shard_map/all_to_all | solution.py:186
  379.5 3.5 copy.56
  382.9 4.4 %reshape.65 = bf16[864,1344]{1,0:T(8,128)(2,1)} reshape(bf16[8,2,54,1344]{3,2,1,0:T(8,128)(2,1)} %copy.56) | data formatting | bytes 4644864 | tf_op jit(solution)/shard_map/reshape | solution.py:188
  387.4 3.0 convolution_convert_fusion.1
  (79 shorter events, 17.0 us)
Async XLA Ops:
  7.2 323.5 %copy-start = (bf16[2688,256]{1,0:T(8,128)(2,1)S(1)}, bf16[2688,256]{1,0:T(8,128)(2,1)}, u32[]{:S(2)}) copy-start(bf16[2688,256]{1,0:T(8,128)(2,1)} %param.25) | copy-start | bytes 4128772
  10.9 0.6 copy-start.10
  52.0 7.5 %copy-start.6 = (f32[2688]{0:T(1024)S(1)}, f32[2688]{0:T(1024)}, u32[]{:S(2)}) copy-start(f32[2688]{0:T(1024)} %param.15) | copy-start | bytes 32260
  52.0 63.0 %all-to-all-start = ((bf16[8,2,54,1344]{3,1,2,0:T(2,128)(2,1)}), bf16[8,2,54,1344]{3,1,2,0:T(2,128)(2,1)}, u32[]{:S(2)}, u32[]{:S(2)}) async-start(bf16[8,2,54,1344]{3,1,2,0:T(2,128)(2,1)} %copy.48), calls=%async_computation | async-start | bytes 4866048 | tf_op jit(solution)/shard_map/all_to_all | solution.py:156
  59.4 233.2 %all-gather.2.cloned.1.call-start = ((), (), s32[]{:S(2)}) async-start(), calls=%async_computation.3 | async-start | bytes 11403264 | tf_op jit(solution)/shard_map/all_gather | solution.py:181
  117.5 1.5 copy-start.1
  120.7 53.9 %collective-permute-start = (bf16[8,2,54,1344]{3,0,2,1:T(8,128)(2,1)}, bf16[8,2,54,1344]{3,0,2,1:T(8,128)(2,1)}, u32[]{:S(2)}, u32[]{:S(2)}) collective-permute-start(bf16[8,2,54,1344]{3,0,2,1:T(8,128)(2,1)} %copy.50), channel_id=1, source_target_pairs={{0,1},{1,0},{2,3},{3,2},{4,5},{5,4},{6,7},{7,6},{8,9},{9,8},{10,11... | collective-permute-start | bytes 6967304 | tf_op jit(solution)/shard_map/ppermute | solution.py:18
  174.6 2.4 copy-start.2
  177.0 10.4 %slice-start = ((s8[9977856]{0:T(1024)(128)(4,1)}), s8[4194304]{0:T(1024)(128)(4,1)S(1)}, s32[]{:S(2)}) async-start(s8[9977856]{0:T(1024)(128)(4,1)} %bitcast.159), calls=%async_computation.5 | async-start | bytes 8388608
  177.0 10.4 %slice-start.1 = ((s8[9977856]{0:T(1024)(128)(4,1)}), s8[4194304]{0:T(1024)(128)(4,1)S(1)}, s32[]{:S(2)}) async-start(s8[9977856]{0:T(1024)(128)(4,1)} %bitcast.159), calls=%async_computation.6 | async-start | bytes 8388608
  181.7 5.7 %slice-start.2 = ((s8[9977856]{0:T(1024)(128)(4,1)}), s8[1589248]{0:T(1024)(128)(4,1)S(1)}, s32[]{:S(2)}) async-start(s8[9977856]{0:T(1024)(128)(4,1)} %bitcast.159), calls=%async_computation.7 | async-start | bytes 3178496
  318.4 6.0 %copy-start.4 = (bf16[1,128,1024]{2,1,0:T(8,128)(2,1)S(1)}, bf16[1,128,1024]{2,1,0:T(8,128)(2,1)}, u32[]{:S(2)}) copy-start(bf16[1,128,1024]{2,1,0:T(8,128)(2,1)} %param.20) | copy-start | bytes 786436
  318.4 6.1 %copy-start.5 = (bf16[1,128,256]{2,1,0:T(8,128)(2,1)S(1)}, bf16[1,128,256]{2,1,0:T(8,128)(2,1)}, u32[]{:S(2)}) copy-start(bf16[1,128,256]{2,1,0:T(8,128)(2,1)} %param.21) | copy-start | bytes 196612
  318.4 6.4 %copy-start.3 = (bf16[1,128,2688]{2,1,0:T(8,128)(2,1)S(1)}, bf16[1,128,2688]{2,1,0:T(8,128)(2,1)}, u32[]{:S(2)}) copy-start(bf16[1,128,2688]{2,1,0:T(8,128)(2,1)} %param.23) | copy-start | bytes 2064388
  318.4 61.0 %all-to-all-start.1 = ((bf16[8,2,54,1344]{3,1,2,0:T(2,128)(2,1)}), bf16[8,2,54,1344]{3,1,2,0:T(2,128)(2,1)}, u32[]{:S(2)}, u32[]{:S(2)}) async-start(bf16[8,2,54,1344]{3,1,2,0:T(2,128)(2,1)} %copy.55), calls=%async_computation.1 | async-start | bytes 4866048 | tf_op jit(solution)/shard_map/all_to_all | solution.py:186
  324.1 32.1 %reduce-scatter.2.cloned.1.call-start = ((), (), s32[]{:S(2)}) async-start(), calls=%async_computation.4 | async-start | bytes 1032192 | tf_op jit(solution)/shard_map/reduce_scatter | solution.py:176
  324.5 4.8 %copy-start.16 = (bf16[1,128,256]{2,1,0:T(8,128)(2,1)S(1)}, bf16[1,128,256]{2,1,0:T(8,128)(2,1)}, u32[]{:S(2)}) copy-start(bf16[1,128,256]{2,1,0:T(8,128)(2,1)} %param.22) | copy-start | bytes 196612
  336.9 2.6 copy-start.7
  356.2 34.2 %collective-permute-start.2 = (bf16[128,1344]{0,1:T(8,128)(2,1)}, bf16[128,1344]{0,1:T(8,128)(2,1)S(1)}, u32[]{:S(2)}, u32[]{:S(2)}) collective-permute-start(bf16[128,1344]{0,1:T(8,128)(2,1)} %reduce-scatter.2.cloned.1.call-done), channel_id=1, source_target_pairs={{0,16},{16,0},{1,17},{17,1},{2,18},{18,2},{3,19},{19,3},{4,20},{20... | collective-permute-start | bytes 1032200 | tf_op jit(solution)/shard_map/ppermute | solution.py:33
  382.9 4.4 %copy-start.9 = (s32[128]{0:T(128)S(1)}, s32[128]{0:T(128)}, u32[]{:S(2)}) copy-start(s32[128]{0:T(128)} %copy-done.8) | copy-start | bytes 1540
  382.9 4.4 %copy-start.11 = (s32[128]{0:T(128)S(1)}, s32[128]{0:T(128)}, u32[]{:S(2)}) copy-start(s32[128]{0:T(128)} %copy-done.10) | copy-start | bytes 1540
  382.9 4.4 %copy-start.13 = (s32[128]{0:T(128)S(1)}, s32[128]{0:T(128)}, u32[]{:S(2)}) copy-start(s32[128]{0:T(128)} %copy-done.12) | copy-start | bytes 1540
  382.9 4.4 %copy-start.15 = (s32[128]{0:T(128)S(1)}, s32[128]{0:T(128)}, u32[]{:S(2)}) copy-start(s32[128]{0:T(128)} %copy-done.14) | copy-start | bytes 1540
  390.4 1.7 collective-permute-start.1
  (3 other events, 1.7 us)
Sparse Core Ops, SparseCore 0:
  197.1 95.4 all-gather.1
  339.6 16.5 reduce-scatter.1
